TPU v7x, 512 devices: a whole 4x8x8 slice. The times are simulated.
512 devices in a mesh: seq: 128 (over y, z, core), mp: 4 (over x).
Axes of the slice: x: 4, y: 8, z: 8, core: 2. Of those that a mesh axis runs over, the one named last changes fastest.
Arguments:
- fresh_queries: bfloat16 [8192, 2048], P('seq', 'mp'), may hold values from -120 to 120
- fresh_keys: bfloat16 [8192, 1024], P('seq', 'mp'), may hold values from -6 to 6
- fresh_values: bfloat16 [8192, 1024], P('seq', 'mp'), may hold values from -6 to 6
- cache: bfloat16 [2, 8192, 1024], P(None, 'seq', 'mp'), may hold values from -6 to 6
- pool_root: int32 [128, 32], replicated, may hold values from 0 to 31
- branch_owner: int32 [128], replicated, may hold values from 0 to 127, each once
- branch_len: int32 [128], replicated, may hold values from 1 to 32, 2048 in all
- branch_root: int32 [128], replicated, may hold values from 0 to 31
- request_branch: int32 [128, 4], P('seq'), may hold values from 0 to 127
- token_request: int32 [128, 64], P('seq'), may hold values from 0 to 3, never falling along the last dimension, each value on 1 to 32 neighbouring positions
- residual: bfloat16 [8192, 2048], P('seq'), may hold values from -1.5 to 1.5
- wo_t: bfloat16 [2048, 2048], P('seq', 'mp'), may hold values from -0.125 to 0.125
- norm_gain: float32 [2048], replicated, may hold values from 0.1 to 1.9
- w_qkv: bfloat16 [2048, 4096], P('seq', 'mp'), may hold values from -0.125 to 0.125
Outputs:
- attn: bfloat16 [8192, 2048], P('seq', 'mp')
- stream: bfloat16 [8192, 2048], P('seq')
- qkv_next: bfloat16 [8192, 4096], P('seq', 'mp')
Inputs may be any that keep to these rules, and one draw needn't show every extreme that they name: `token_request`: in each index's row the request number never falls, and each request has 1 to 32 tokens. `branch_owner`: each index of seq holds exactly one branch. `branch_len`: the longest branch has 32 rows.
All inputs are finite; a program needn't handle non-finite values.
Results may differ from a plain program's by a relative error of at most 0.018.
Values may be sent and summed in bfloat16 or wider, within the bound.
A program may use at most 64 MiB of HBM per device.

v0:
```python
import jax
import jax.numpy as jnp
from jax import lax
from jax.sharding import PartitionSpec as P

QUERY_HEADS = 16
KEY_VALUE_HEADS = 8
HEAD_SIZE = 128


def cache_tags(pool_root, branch_owner, branch_len, root_count, slot_count):
    owner_count = pool_root.shape[0]
    branch_count = branch_owner.shape[0]
    branch_ids = jnp.arange(branch_count, dtype=jnp.int32)
    owner_ids = jnp.arange(owner_count, dtype=jnp.int32)
    owned = jnp.sum(
        jnp.where(branch_owner[None, :] == owner_ids[:, None], branch_ids[None, :], 0), axis=1
    )
    owned_length = jnp.sum(
        jnp.where(branch_ids[None, :] == owned[:, None], branch_len[None, :], 0), axis=1
    )
    slot_ids = jnp.arange(slot_count, dtype=jnp.int32)
    branch_tags = jnp.where(
        slot_ids[None, :] < owned_length[:, None], root_count + owned[:, None], -1
    )
    return jnp.concatenate([pool_root, branch_tags], axis=1).reshape(-1)


def absorb(running, query_rows, key_row_block, value_rows, visible, score_scale):
    peak_old, total, mixed = running
    scores = (
        jnp.einsum("tkgd,rkd->tkgr", query_rows, key_row_block, preferred_element_type=jnp.float32)
        * score_scale
    )
    seen = visible[:, None, None, :]
    peak_new = jnp.maximum(peak_old, jnp.max(jnp.where(seen, scores, -jnp.inf), axis=-1))
    factor = jnp.exp(peak_old - peak_new)
    weights_full = jnp.where(seen, jnp.exp(scores - peak_new[..., None]), 0.0)
    total = total * factor + jnp.sum(weights_full, axis=-1)
    mixed = mixed * factor[..., None] + jnp.einsum(
        "tkgr,rkd->tkgd",
        weights_full.astype(jnp.bfloat16),
        value_rows,
        preferred_element_type=jnp.float32,
    )
    return (peak_new, total, mixed)


def on_device(
    fresh_queries,
    fresh_keys,
    fresh_values,
    cache,
    pool_root,
    branch_owner,
    branch_len,
    branch_root,
    request_branch,
    token_request,
    residual,
    wo_t,
    norm_gain,
    w_qkv,
):
    seq_count = lax.axis_size("seq")
    root_count = seq_count // 4
    tok_rows = fresh_queries.shape[0]
    kv_local = fresh_keys.shape[1] // HEAD_SIZE
    query_groups = QUERY_HEADS // KEY_VALUE_HEADS
    score_scale = HEAD_SIZE ** (-0.5)
    slot_count = cache.shape[1] - pool_root.shape[1]
    tags = cache_tags(pool_root, branch_owner, branch_len, root_count, slot_count)
    requests = token_request[0]
    local_branches = request_branch[0]
    request_ids = jnp.arange(local_branches.shape[0], dtype=jnp.int32)
    token_branch = jnp.sum(
        jnp.where(requests[:, None] == request_ids[None, :], local_branches[None, :], 0), axis=1
    )
    branch_ids = jnp.arange(branch_root.shape[0], dtype=jnp.int32)
    token_root = jnp.sum(
        jnp.where(token_branch[:, None] == branch_ids[None, :], branch_root[None, :], 0), axis=1
    )
    query_rows = fresh_queries.reshape(tok_rows, kv_local, query_groups, HEAD_SIZE)
    incoming_keys = fresh_keys.reshape(tok_rows, kv_local, HEAD_SIZE)
    incoming_values = fresh_values.reshape(tok_rows, kv_local, HEAD_SIZE)
    positions = jnp.arange(tok_rows, dtype=jnp.int32)
    own_visible = (requests[None, :] == requests[:, None]) & (
        positions[None, :] <= positions[:, None]
    )
    start_state = (
        jnp.full((tok_rows, kv_local, query_groups), -jnp.inf, jnp.float32),
        jnp.zeros((tok_rows, kv_local, query_groups), jnp.float32),
        jnp.zeros((tok_rows, kv_local, query_groups, HEAD_SIZE), jnp.float32),
    )
    start_state = absorb(
        start_state, query_rows, incoming_keys, incoming_values, own_visible, score_scale
    )
    state = start_state
    piece = lax.all_gather(cache, "seq", axis=1, tiled=True)
    rows = piece.shape[1]
    block = 512
    key_blocks = piece[0].reshape(rows // block, block, kv_local, HEAD_SIZE)
    value_blocks = piece[1].reshape(rows // block, block, kv_local, HEAD_SIZE)
    tag_blocks = tags.reshape(rows // block, block)

    def one_block(running, parts):
        key_row_block, value_rows, tag_rows = parts
        visible = (tag_rows[None, :] == token_root[:, None]) | (
            tag_rows[None, :] == root_count + token_branch[:, None]
        )
        updated = absorb(running, query_rows, key_row_block, value_rows, visible, score_scale)
        return (updated, None)

    state, unused = lax.scan(one_block, state, (key_blocks, value_blocks, tag_blocks))
    peak_final, total_final, mixed_final = state
    attn = (
        (mixed_final / total_final[..., None])
        .reshape(tok_rows, kv_local * query_groups * HEAD_SIZE)
        .astype(jnp.bfloat16)
    )
    partial_value = lax.dot_general(
        attn,
        lax.all_gather(wo_t, "seq", axis=0, tiled=True),
        (((1,), (1,)), ((), ())),
        preferred_element_type=jnp.float32,
    )
    summed = lax.psum(partial_value.astype(jnp.bfloat16), "mp").astype(jnp.float32)
    stream = (residual.astype(jnp.float32) + summed).astype(jnp.bfloat16)
    widened = stream.astype(jnp.float32)
    mean_square = jnp.mean(widened * widened, axis=-1, keepdims=True)
    normed = (widened * lax.rsqrt(mean_square + 1e-06) * norm_gain[None, :]).astype(jnp.bfloat16)
    qkv_sum = jnp.dot(
        normed, lax.all_gather(w_qkv, "seq", axis=0, tiled=True), preferred_element_type=jnp.float32
    )
    return (attn, stream, qkv_sum.astype(jnp.bfloat16))


def solution(mesh):
    return jax.shard_map(
        on_device,
        mesh=mesh,
        in_specs=(
            P("seq", "mp"),
            P("seq", "mp"),
            P("seq", "mp"),
            P(None, "seq", "mp"),
            P(),
            P(),
            P(),
            P(),
            P("seq", None),
            P("seq", None),
            P("seq", None),
            P("seq", "mp"),
            P(),
            P("seq", "mp"),
        ),
        out_specs=(P("seq", "mp"), P("seq", None), P("seq", "mp")),
        check_vma=False,
    )
```

profile of v0, /device:TPU:1, one launch (start us, length us, event | category | flops | bytes accessed | tf_op | source)
XLA Modules:
  0.0 339.6 jit_solution(17679690994480268077)
XLA Ops:
  16.6 88.7 %all-gather.4.cloned.1.call-done = bf16[2,8192,256]{2,1,0:T(8,128)(2,1)} async-done(((bf16[2,64,256]{2,1,0:T(8,128)(2,1)}), bf16[2,8192,256]{2,1,0:T(8,128)(2,1)}) %all-gather.4.cloned.1.call-update) | async-done | bytes 8388624 | tf_op jit(solution)/shard_map/all_gather | solution.py:99
  105.3 5.7 %fusion.30 = (bf16[1,8192,256]{2,1,0:T(8,128)(2,1)}, bf16[1,8192,256]{2,1,0:T(8,128)(2,1)}) fusion(bf16[2,8192,256]{2,1,0:T(8,128)(2,1)} %all-gather.4.cloned.1.call-done), kind=kLoop, calls=%fused_computation.64 | loop fusion | bytes 16777216 | tf_op jit(solution)/shard_map/slice | solution.py:103
  111.0 6.9 %reshape.143 = bf16[16,512,2,128]{3,2,1,0:T(2,128)(2,1)} reshape(bf16[1,8192,256]{2,1,0:T(8,128)(2,1)} %get-tuple-element.107) | data formatting | bytes 8388608 | tf_op jit(solution)/shard_map/reshape;squeeze | solution.py:102
  118.0 6.9 %reshape.144 = bf16[16,512,2,128]{3,2,1,0:T(2,128)(2,1)} reshape(bf16[1,8192,256]{2,1,0:T(8,128)(2,1)} %get-tuple-element.106) | data formatting | bytes 8388608 | tf_op jit(solution)/shard_map/reshape;squeeze | solution.py:103
  124.9 39.2 %while.14 = (s32[]{:T(128)}, f32[64,2,2]{0,2,1:T(2,128)S(1)}, f32[64,2,2]{0,2,1:T(2,128)S(1)}, f32[64,2,2,128]{3,0,2,1:T(8,128)S(1)}, s32[16,512]{1,0:T(8,128)S(...) while((s32[]{:T(128)}, f32[64,2,2]{0,2,1:T(2,128)S(1)}, ...), condition=%wide.region_9.10_spmd, body=%wide.region_6.9_spmd.sunk | while | flops 68452928 | bytes 3628149 | solution.py:114
  125.0 1.4 constant_dynamic-slice_fusion.6
  127.5 1.4 constant_dynamic-slice_fusion.6
  129.9 1.4 constant_dynamic-slice_fusion.6
  132.4 1.4 constant_dynamic-slice_fusion.6
  134.8 1.4 constant_dynamic-slice_fusion.6
  137.3 1.4 constant_dynamic-slice_fusion.6
  139.7 1.4 constant_dynamic-slice_fusion.6
  142.2 1.4 constant_dynamic-slice_fusion.6
  144.6 1.4 constant_dynamic-slice_fusion.6
  147.1 1.4 constant_dynamic-slice_fusion.6
  149.5 1.4 constant_dynamic-slice_fusion.6
  152.0 1.4 constant_dynamic-slice_fusion.6
  154.4 1.4 constant_dynamic-slice_fusion.6
  159.3 1.4 constant_dynamic-slice_fusion.6
  164.3 23.8 %all-gather.6.cloned.1.call-done = bf16[2048,512]{1,0:T(8,128)(2,1)} async-done(((bf16[16,512]{1,0:T(8,128)(2,1)}), bf16[2048,512]{1,0:T(8,128)(2,1)}) %all-gather.6.cloned.1.call-update) | async-done | bytes 2097168 | tf_op jit(solution)/shard_map/all_gather | solution.py:123
  188.1 3.0 convolution_convert_fusion
  191.8 46.3 %all-reduce.2.cloned.1.call-done = bf16[64,2048]{1,0:T(8,128)(2,1)} async-done(((bf16[64,2048]{1,0:T(8,128)(2,1)}), bf16[64,2048]{1,0:T(8,128)(2,1)}) %all-reduce.2.cloned.1.call-update) | async-done | bytes 262160 | tf_op jit(solution)/shard_map/psum | solution.py:127
  239.3 90.1 %all-gather.8.cloned.1.call-done = bf16[2048,1024]{1,0:T(8,128)(2,1)} async-done(((bf16[16,1024]{1,0:T(8,128)(2,1)}), bf16[2048,1024]{1,0:T(8,128)(2,1)}) %all-gather.8.cloned.1.call-update) | async-done | bytes 4194320 | tf_op jit(solution)/shard_map/all_gather | solution.py:133
  329.3 3.7 %convolution_convert_fusion.1 = bf16[64,1024]{1,0:T(8,128)(2,1)} fusion(bf16[2048,1024]{1,0:T(8,128)(2,1)} %all-gather.8.cloned.1.call-done, bf16[64,2048]{1,0:T(8,128)(2,1)S(1)} %get-tuple-element.101, f32[2048]{0:T(1024)S(1)} %copy-done.3, f32[64]{0:T(128)S(1)} %add_rsqrt_fusion), kind=kOutput, calls=%fused_computation.22 | convolution fusion | flops 269025280 | bytes 4595968 | tf_op jit(solution)/shard_map/dot_general | solution.py:132
  (185 shorter events, 29.8 us)
Async XLA Ops:
  7.2 98.1 %all-gather.4.cloned.1.call-start = ((), (), s32[]{:S(2)}) async-start(), calls=%async_computation | async-start | bytes 8454144 | tf_op jit(solution)/shard_map/all_gather | solution.py:99
  7.9 180.2 %all-gather.6.cloned.1.call-start = ((), (), s32[]{:S(2)}) async-start(), calls=%async_computation.1 | async-start | bytes 2113536 | tf_op jit(solution)/shard_map/all_gather | solution.py:123
  8.6 229.4 %all-reduce.2.cloned.1.call-start = ((), (), s32[]{:S(2)}) async-start(), calls=%async_computation.2 | async-start | bytes 524288 | tf_op jit(solution)/shard_map/psum | solution.py:127
  124.9 113.2 %copy-start.2 = (bf16[64,2048]{1,0:T(8,128)(2,1)S(1)}, bf16[64,2048]{1,0:T(8,128)(2,1)}, u32[]{:S(2)}) copy-start(bf16[64,2048]{1,0:T(8,128)(2,1)} %param.26) | copy-start | bytes 786436
  124.9 204.4 %copy-start.3 = (f32[2048]{0:T(1024)S(1)}, f32[2048]{0:T(1024)}, u32[]{:S(2)}) copy-start(f32[2048]{0:T(1024)} %param.28) | copy-start | bytes 24580
  164.3 168.7 %copy-start.1 = (bf16[64,512]{1,0:T(8,128)(2,1)}, bf16[64,512]{1,0:T(8,128)(2,1)S(1)}, u32[]{:S(2)}) copy-start(bf16[64,512]{1,0:T(8,128)(2,1)S(1)} %convert_element_type.35) | copy-start | bytes 196612
  191.2 138.1 %all-gather.8.cloned.1.call-start = ((), (), s32[]{:S(2)}) async-start(), calls=%async_computation.3 | async-start | bytes 4227072 | tf_op jit(solution)/shard_map/all_gather | solution.py:133
  239.2 93.8 %copy-start = (bf16[64,2048]{1,0:T(8,128)(2,1)}, bf16[64,2048]{1,0:T(8,128)(2,1)S(1)}, u32[]{:S(2)}) copy-start(bf16[64,2048]{1,0:T(8,128)(2,1)S(1)} %get-tuple-element.101) | copy-start | bytes 786436
Sparse Core Ops, SparseCore 0:
  11.2 94.0 all-gather.3
  108.4 79.6 all-gather.5
  191.3 46.7 all-reduce.1
  241.5 87.7 all-gather.7
where the time goes:
time: 341 us; the launch traced here: 340 us
  waiting for transfers between devices  251 us (74%)
  local copies, waits for them, and re-layouts  44.9 us (13%)
  matrix products  17.1 us (5%)
  between operations  13.9 us (4%)
  other arithmetic  11.8 us (3%)
    all_gather x1, waiting for transfers between devices, on_device(): lax.all_gather(w_qkv, 'seq', axis=0, tiled=True)  90.1 us
    all_gather x1, waiting for transfers between devices, on_device(): piece = lax.all_gather(cache, 'seq', axis=1, tiled=True)  88.7 us
    psum x1, waiting for transfers between devices, on_device(): lax.psum(partial_value.astype(jnp.bfloat16), 'mp').astype(jnp.float32)  46.3 us
    all_gather x1, waiting for transfers between devices, on_device(): lax.all_gather(wo_t, 'seq', axis=0, tiled=True)  23.8 us
    dynamic_slice x32, local copies, waits for them, and re-layouts, on_device(): lax.scan(one_block, state, (key_blocks, value_blocks, tag_blocks))  22.5 us
    another operation x1, local copies, waits for them, and re-layouts, on_device(): value_blocks = piece[1].reshape(rows // block, block, kv_local, HEAD_SIZE)  6.94 us
    another operation x1, local copies, waits for them, and re-layouts, on_device(): key_blocks = piece[0].reshape(rows // block, block, kv_local, HEAD_SIZE)  6.93 us
  transfers between devices with their start and end apart: 4, of which 4 were waited for; matrix products, arithmetic and copies ran while one was open for 20% of the time, Pallas kernels for 0%

commit v1 on v0

v1 whole, which is shorter than its diff:
```python
import math

import jax
import jax.numpy as jnp
from jax import lax
from jax.experimental import pallas as pl
from jax.experimental.pallas import tpu as pltpu
from jax.sharding import PartitionSpec as P

HEAD = 128
RING = 8
HALFRING = RING // 2
ROOTS = 32
ROWS = 160
NEG = -1e30
MESH = pl.DeviceIdType.MESH
F32 = jnp.float32
BF16 = jnp.bfloat16


def kernel(
    q_ref, fk_ref, fv_ref, cache_ref, pool_ref, owner_ref, len_ref, broot_ref, rb_ref, tr_ref,
    res_ref, wo_ref, gain_ref, wq_ref,
    attn_ref, stream_ref, qkv_ref,
    kvg, wqg, qb, s3, mx, mrun, acc, tags, tagc, rootb, brb, part, rsb, normed, qacc,
    send1, send2, recv1, recv2, part1, part2, xsend, xrecv,
):
    seq = lax.axis_index("seq")
    x = lax.axis_index("mp")
    y, z, c = seq // 16, (seq // 2) % RING, seq % 2
    scale2 = HEAD ** (-0.5) * math.log2(math.e)

    def dev(yy, zz, cc):
        return {"seq": (yy * RING + zz) * 2 + cc}

    def xdev(xx):
        return {"mp": xx}

    mate = dev(y, z, 1 - c)
    sec = (z, y)
    prim = (y, z)

    def place(h, ss, pp):
        return (pp, ss) if h == 0 else (ss, pp)

    def at(h, ss, pp):
        yy, zz = place(h, ss, pp)
        return dev(yy, zz, c)

    barrier = pltpu.get_barrier_semaphore()

    def greet(d, carry):
        pl.semaphore_signal(barrier, inc=1, device_id=dev((y + d) % RING, z, c), device_id_type=MESH)
        pl.semaphore_signal(barrier, inc=1, device_id=dev(y, (z + d) % RING, c), device_id_type=MESH)
        return carry

    lax.fori_loop(1, RING, greet, 0)
    pl.semaphore_signal(barrier, inc=1, device_id=mate, device_id_type=MESH)
    for d in range(1, 4):
        pl.semaphore_signal(barrier, inc=1, device_id=xdev((x + d) % 4), device_id_type=MESH)

    for h in range(2):
        kvg[h, seq, 0:64, :] = cache_ref[0, :, h * HEAD:(h + 1) * HEAD]
        kvg[h, seq, 64:128, :] = cache_ref[1, :, h * HEAD:(h + 1) * HEAD]
        for g in range(2):
            j = 2 * h + g
            kvg[h, seq, 128 + 16 * g:144 + 16 * g, :] = wo_ref[:, j * HEAD:(j + 1) * HEAD]
            qb[h, g * 64:(g + 1) * 64, :] = q_ref[:, j * HEAD:(j + 1) * HEAD]
        wqg[h, seq] = wq_ref[:, h * 512:(h + 1) * 512]

    e_id = lax.broadcasted_iota(jnp.int32, (128, 128), 0)
    b_id = lax.broadcasted_iota(jnp.int32, (128, 128), 1)
    owns = owner_ref[...] == e_id
    owned = jnp.sum(jnp.where(owns, b_id.astype(F32), 0.0), axis=1, keepdims=True)
    olen = jnp.sum(jnp.where(owns, len_ref[...].astype(F32), 0.0), axis=1, keepdims=True)
    slot = lax.broadcasted_iota(jnp.int32, (128, 32), 1).astype(F32)
    btag = jnp.where(slot < olen, ROOTS + owned, -1.0)
    pool = pool_ref[...].astype(F32)
    tags[...] = jnp.concatenate([pool, btag, pool, btag], axis=1)
    even = tags[pl.ds(0, 64, stride=2), :]
    odd = tags[pl.ds(1, 64, stride=2), :]
    lane = lax.broadcasted_iota(jnp.int32, (64, 128), 1)
    tagc[...] = jnp.where(lane < 64, even, odd)

    pl.semaphore_wait(barrier, 2 * (RING - 1) + 1 + 3)

    def copy1(h, yy, zz, cc, sem, to):
        ref = kvg.at[h, (yy * RING + zz) * 2 + cc]
        return pltpu.make_async_remote_copy(
            src_ref=ref, dst_ref=ref, send_sem=send1.at[h], recv_sem=sem.at[h, yy, zz],
            device_id=to, device_id_type=MESH)

    def copy2(h, yy, zz, cc, sem, to):
        ref = wqg.at[h, (yy * RING + zz) * 2 + cc]
        return pltpu.make_async_remote_copy(
            src_ref=ref, dst_ref=ref, send_sem=send2.at[h], recv_sem=sem.at[h, yy, zz],
            device_id=to, device_id_type=MESH)

    def inject(copy, rsem, psem, h, pp):
        yy, zz = place(h, sec[h], pp)
        copy(h, yy, zz, c, rsem, at(h, (sec[h] + 1) % RING, prim[h])).start()
        copy(h, yy, zz, c, rsem, at(h, (sec[h] + RING - 1) % RING, prim[h])).start()
        copy(h, yy, zz, c, psem, mate).start()

    def first(copy, rsem):
        def body(d, carry):
            for h in range(2):
                copy(h, y, z, c, rsem, at(h, sec[h], (prim[h] + d) % RING)).start()
            return carry
        return body

    lax.fori_loop(1, RING, first(copy1, recv1), 0)
    for h in range(2):
        inject(copy1, recv1, part1, h, prim[h])
    lax.fori_loop(1, RING, first(copy2, recv2), 0)

    tr = tr_ref[...].astype(F32)
    t_id = lax.broadcasted_iota(jnp.int32, (64, 64), 0)
    u_id = lax.broadcasted_iota(jnp.int32, (64, 64), 1)
    trc = jnp.sum(jnp.where(t_id == u_id, tr, 0.0), axis=1, keepdims=True)
    rb = rb_ref[...].astype(F32)
    tb = jnp.zeros((64, 1), F32)
    for r in range(4):
        tb = jnp.where(trc == float(r), rb[:, r:r + 1], tb)
    troot = jnp.sum(
        jnp.where(tb == lane.astype(F32), broot_ref[...].astype(F32), 0.0), axis=1, keepdims=True)
    rootb[...] = jnp.broadcast_to(troot, (64, 128))
    brb[...] = jnp.broadcast_to(tb + ROOTS, (64, 128))
    own_seen = (tr == trc) & (u_id <= t_id)
    own_seen2 = jnp.concatenate([own_seen.astype(F32), own_seen.astype(F32)], axis=0) > 0.5
    ones64 = jnp.ones((64, HEAD), BF16)
    for h in range(2):
        s = lax.dot_general(
            qb[h], fk_ref[:, h * HEAD:(h + 1) * HEAD], (((1,), (1,)), ((), ())),
            preferred_element_type=F32)
        s = jnp.where(own_seen2, s, NEG)
        m = jnp.max(s, axis=1, keepdims=True)
        p = jnp.exp2((s - m) * scale2).astype(BF16)
        v = jnp.concatenate([fv_ref[:, h * HEAD:(h + 1) * HEAD], ones64], axis=1)
        acc[h] = jnp.dot(p, v, preferred_element_type=F32)
        mrun[h] = jnp.broadcast_to(m, (128, 128))
        mx[h] = jnp.full((128, 128), NEG, F32)

    def wait_same(copy, rsem, h, yy, zz):
        copy(h, yy, zz, c, rsem, mate).wait_recv()

    def wait_mate(copy, psem, h, yy, zz):
        copy(h, yy, zz, 1 - c, psem, mate).wait_recv()

    def inject_rest(copy, rsem, psem):
        def body(i, carry):
            d = jnp.where(i % 2 == 1, (i + 1) // 2, RING - i // 2)
            for h in range(2):
                pp = (prim[h] + d) % RING
                yy, zz = place(h, sec[h], pp)
                wait_same(copy, rsem, h, yy, zz)
                inject(copy, rsem, psem, h, pp)
            return carry
        return body

    lax.fori_loop(1, RING, inject_rest(copy1, recv1, part1), 0)

    def relay(copy, rsem, psem, step, b):
        for h in range(2):
            if step == HALFRING:
                yy, zz = place(h, (sec[h] + HALFRING) % RING, b)
                wait_same(copy, rsem, h, yy, zz)
                copy(h, yy, zz, c, psem, mate).start()
                continue
            for way in (1, -1):
                yy, zz = place(h, (sec[h] - way * step + RING) % RING, b)
                wait_same(copy, rsem, h, yy, zz)
                onward = at(h, (sec[h] + way + RING) % RING, prim[h])
                if step < HALFRING - 1:
                    copy(h, yy, zz, c, rsem, onward).start()
                else:
                    @pl.when(b % 2 == (0 if way == 1 else 1))
                    def _():
                        copy(h, yy, zz, c, rsem, onward).start()
                copy(h, yy, zz, c, psem, mate).start()

    def bundle(h, step, b):
        if step == 0:
            return [place(h, sec[h], b)]
        if step == HALFRING:
            return [place(h, (sec[h] + HALFRING) % RING, b)]
        return [place(h, (sec[h] - step + RING) % RING, b), place(h, (sec[h] + step) % RING, b)]

    def qk(step, b):
        for h in range(2):
            slots = bundle(h, step, b)
            keys = []
            for yy, zz in slots:
                wait_mate(copy1, part1, h, yy, zz)
            for yy, zz in slots:
                keys.append(kvg[h, pl.ds((yy * RING + zz) * 2, 2), 0:64, :].reshape(128, HEAD))
            k = jnp.concatenate(keys, axis=0) if len(keys) > 1 else keys[0]
            s = lax.dot_general(qb[h], k, (((1,), (1,)), ((), ())), preferred_element_type=F32)
            top = mx[h]
            for i, (yy, zz) in enumerate(slots):
                tag = tagc[pl.ds(yy * RING + zz, 1), :]
                seen = (tag == rootb[...]) | (tag == brb[...])
                si = s[:, i * 128:(i + 1) * 128]
                lo = jnp.where(seen, si[0:64], NEG)
                hi = jnp.where(seen, si[64:128], NEG)
                si = jnp.concatenate([lo, hi], axis=0)
                s3[h, yy, zz] = si
                top = jnp.maximum(top, si)
            mx[h] = top

    def settle():
        for h in range(2):
            old = mrun[h]
            new = jnp.maximum(old, jnp.max(mx[h], axis=1, keepdims=True))
            factor = jnp.exp2((old - new) * scale2)
            mrun[h] = new
            acc[h] = acc[h] * jnp.concatenate([factor, factor], axis=1)

    def pv(step, b):
        for h in range(2):
            slots = bundle(h, step, b)
            m = mrun[h]
            ps, vs = [], []
            for yy, zz in slots:
                ps.append(jnp.exp2((s3[h, yy, zz] - m) * scale2).astype(BF16))
                vs.append(kvg[h, pl.ds((yy * RING + zz) * 2, 2), 64:128, :].reshape(128, HEAD))
            p = jnp.concatenate(ps, axis=1) if len(ps) > 1 else ps[0]
            v = jnp.concatenate(vs, axis=0) if len(vs) > 1 else vs[0]
            v = jnp.concatenate([v, jnp.ones(v.shape, BF16)], axis=1)
            acc[h] += jnp.dot(p, v, preferred_element_type=F32)

    def stage(relays, qk_step, pv_step):
        def body(b, carry):
            if relays is not None:
                relay(*relays, b)
            if qk_step is not None:
                qk(qk_step, b)
            if pv_step is not None:
                pv(pv_step, b)
            return carry
        lax.fori_loop(0, RING, body, 0)

    one = (copy1, recv1, part1)
    two = (copy2, recv2, part2)
    stage((*one, 1), 0, None)
    settle()
    stage((*one, 2), 1, 0)
    settle()
    stage((*one, 3), 2, 1)
    settle()
    for h in range(2):
        inject(*two, h, prim[h])
    lax.fori_loop(1, RING, inject_rest(*two), 0)
    stage((*one, 4), 3, 2)
    settle()
    stage((*two, 1), 4, 3)
    settle()
    stage((*two, 2), None, 4)

    for h in range(2):
        a = (acc[h, :, 0:HEAD] / acc[h, :, HEAD:2 * HEAD]).astype(BF16)
        for g in range(2):
            j = 2 * h + g
            attn_ref[:, j * HEAD:(j + 1) * HEAD] = a[g * 64:(g + 1) * 64]

    def project(yy, carry):
        w = [kvg[h, pl.ds(yy * 16, 16), 128 + 16 * g:144 + 16 * g, :].reshape(256, HEAD)
             for h in range(2) for g in range(2)]
        t = lax.dot_general(
            attn_ref[...], jnp.concatenate(w, axis=1), (((1,), (1,)), ((), ())),
            preferred_element_type=F32)
        part[:, pl.ds(pl.multiple_of(yy * 256, 256), 256)] = t.astype(BF16)
        return carry

    lax.fori_loop(0, RING, project, 0)

    def rows(xx):
        return pl.ds(pl.multiple_of(xx * 16, 16), 16)

    def scatter(d):
        xx = (x + d) % 4
        return pltpu.make_async_remote_copy(
            src_ref=part.at[rows(xx)], dst_ref=rsb.at[4 - d - 1], send_sem=xsend.at[0, d - 1],
            recv_sem=xrecv.at[0, 4 - d - 1], device_id=xdev(xx), device_id_type=MESH)

    for d in (2, 1, 3):
        scatter(d).start()
    stage((*two, 3), None, None)
    total = part[rows(x), :].astype(F32)
    for d in range(1, 4):
        scatter(4 - d).wait_recv()
        total = total + rsb[d - 1].astype(F32)
    stream_ref[rows(x), :] = (res_ref[rows(x), :].astype(F32) + total).astype(BF16)

    def spread(d, xx):
        return pltpu.make_async_remote_copy(
            src_ref=stream_ref.at[rows(xx)], dst_ref=stream_ref.at[rows(xx)],
            send_sem=xsend.at[1, d - 1], recv_sem=xrecv.at[1, 4 - d - 1],
            device_id=xdev((x + d) % 4), device_id_type=MESH)

    for d in (2, 1, 3):
        spread(d, x).start()
    stage((*two, 4), None, None)
    for d in range(1, 4):
        spread(4 - d, (x + d) % 4).wait_recv()

    wide = stream_ref[...].astype(F32)
    mean = jnp.mean(wide * wide, axis=1, keepdims=True)
    normed[...] = (wide * lax.rsqrt(mean + 1e-06) * gain_ref[...]).astype(BF16)
    qacc[...] = jnp.zeros_like(qacc)

    def qkv(yy, carry):
        n = normed[:, pl.ds(pl.multiple_of(yy * 256, 256), 256)]
        for h in range(2):
            for zz in range(RING):
                wait_mate(copy2, part2, h, yy, zz)
            qacc[:, h * 512:(h + 1) * 512] += jnp.dot(
                n, wqg[h, pl.ds(yy * 16, 16)].reshape(256, 512), preferred_element_type=F32)
        return carry

    lax.fori_loop(0, RING, qkv, 0)
    qkv_ref[...] = qacc[...].astype(BF16)

    for d in range(1, 4):
        scatter(d).wait_send()
        spread(d, x).wait_send()
    for h in range(2):
        for buf, sem in ((kvg, send1), (wqg, send2)):
            sent = buf.at[h, 0:127]
            pltpu.make_async_remote_copy(
                src_ref=sent, dst_ref=sent, send_sem=sem.at[h], recv_sem=recv1.at[h, 0, 0],
                device_id=mate, device_id_type=MESH).wait_send()


def on_device(
    fresh_queries, fresh_keys, fresh_values, cache, pool_root, branch_owner, branch_len,
    branch_root, request_branch, token_request, residual, wo_t, norm_gain, w_qkv,
):
    vmem = pl.BlockSpec(memory_space=pltpu.VMEM)
    args = (
        fresh_queries, fresh_keys, fresh_values, cache, pool_root, branch_owner.reshape(1, -1),
        branch_len.reshape(1, -1), branch_root.reshape(1, -1), request_branch, token_request,
        residual, wo_t, norm_gain.reshape(1, -1), w_qkv,
    )
    dma = pltpu.SemaphoreType.DMA
    return pl.pallas_call(
        kernel,
        out_shape=(
            jax.ShapeDtypeStruct((64, 512), BF16),
            jax.ShapeDtypeStruct((64, 2048), BF16),
            jax.ShapeDtypeStruct((64, 1024), BF16),
        ),
        in_specs=[vmem] * len(args),
        out_specs=(vmem, vmem, vmem),
        scratch_shapes=[
            pltpu.VMEM((2, 2 * RING * RING, ROWS, HEAD), BF16),
            pltpu.VMEM((2, 2 * RING * RING, 16, 512), BF16),
            pltpu.VMEM((2, 128, HEAD), BF16),
            pltpu.VMEM((2, RING, RING, 128, 128), F32),
            pltpu.VMEM((2, 128, 128), F32),
            pltpu.VMEM((2, 128, 128), F32),
            pltpu.VMEM((2, 128, 256), F32),
            pltpu.VMEM((128, 128), F32),
            pltpu.VMEM((64, 128), F32),
            pltpu.VMEM((64, 128), F32),
            pltpu.VMEM((64, 128), F32),
            pltpu.VMEM((64, 2048), BF16),
            pltpu.VMEM((3, 16, 2048), BF16),
            pltpu.VMEM((64, 2048), BF16),
            pltpu.VMEM((64, 1024), F32),
            dma((2,)),
            dma((2,)),
            dma((2, RING, RING)),
            dma((2, RING, RING)),
            dma((2, RING, RING)),
            dma((2, RING, RING)),
            dma((2, 3)),
            dma((2, 3)),
        ],
        compiler_params=pltpu.CompilerParams(
            collective_id=0, has_side_effects=True, vmem_limit_bytes=60 * 1024 * 1024),
    )(*args)


def solution(mesh):
    return jax.shard_map(
        on_device,
        mesh=mesh,
        in_specs=(
            P("seq", "mp"),
            P("seq", "mp"),
            P("seq", "mp"),
            P(None, "seq", "mp"),
            P(),
            P(),
            P(),
            P(),
            P("seq", None),
            P("seq", None),
            P("seq", None),
            P("seq", "mp"),
            P(),
            P("seq", "mp"),
        ),
        out_specs=(P("seq", "mp"), P("seq", None), P("seq", "mp")),
        check_vma=False,
    )
```

time: 341 us -> 89.5 us (0.26)
  the two profiles are of different devices: /device:TPU:1 before, /device:TPU:16 now
where the time goes in v1:
time: 89.5 us; the launch traced here: 89.2 us
  Pallas kernels  83.3 us (93%)
  local copies, waits for them, and re-layouts  5.28 us (6%)
    pallas_call x1, Pallas kernels, on_device(): pl.pallas_call(kernel, out_shape=(jax.ShapeDtypeStruct((64, 512), BF16),...  83.3 us
    unnamed x6, local copies, waits for them, and re-layouts  5.28 us

profile of v1, /device:TPU:16, one launch (start us, length us, event | category | flops | bytes accessed | tf_op | source)
XLA Modules:
  0.0 89.2 jit_solution(11609760159155206971)
XLA Ops:
  0.6 1.4 %copy.17.pool_ref = s32[128,32]{1,0:T(8,128)} copy(s32[128,32]{0,1:T(8,128)} %param.18) | data formatting | bytes 32768 | tf_op args[4]
  2.1 83.3 %shard_map.157 = (bf16[64,512]{1,0:T(8,128)(2,1)}, bf16[64,2048]{1,0:T(8,128)(2,1)}, bf16[64,1024]{1,0:T(8,128)(2,1)}) custom-call(bf16[64,512]{1,0:T(8,128)(2,1)} %q_ref.1, bf16[64,256]{1,0:T(8,128)(2,1)} %fk_ref.1, bf16[64,256]{1,0:T(8,128)(2,1)} %fv_ref.1, bf16[2,64,256]{2,1,0:T(8,128)(2,1)} %cache_ref.1, s32[128,32]{1,0:T(8,128)} %copy.17.pool_ref, ...), custom_call_target="tpu_custom_call" | custom-call | tf_op jit(solution)/shard_map/pallas_call | solution.py:346
  85.4 1.5 %copy.21 = bf16[64,512]{1,0:T(8,128)(2,1)} copy(bf16[64,512]{1,0:T(8,128)(2,1)} %get-tuple-element.6) | data formatting | bytes 131072
  86.9 0.0 copy-start
  86.9 1.7 %copy.22 = bf16[64,2048]{1,0:T(8,128)(2,1)} copy(bf16[64,2048]{1,0:T(8,128)(2,1)} %get-tuple-element.7) | data formatting | bytes 524288
  88.6 0.0 copy-done
  88.6 0.7 copy.23
Async XLA Ops:
  86.9 1.7 %copy-start = (bf16[64,1024]{1,0:T(8,128)(2,1)S(1)}, bf16[64,1024]{1,0:T(8,128)(2,1)}, u32[]{:S(2)}) copy-start(bf16[64,1024]{1,0:T(8,128)(2,1)} %get-tuple-element.8) | copy-start | bytes 393220

commit v2 on v1

v2 whole, which is shorter than its diff:
```python
import math

import jax
import jax.numpy as jnp
from jax import lax
from jax.experimental import pallas as pl
from jax.experimental.pallas import tpu as pltpu
from jax.sharding import PartitionSpec as P

HEAD = 128
RING = 8
HALFRING = RING // 2
ROOTS = 32
ROWS = 160
NEG = -1e30
FLOOR = -1e9
MESH = pl.DeviceIdType.MESH
F32 = jnp.float32
BF16 = jnp.bfloat16


def kernel(
    q_ref, fk_ref, fv_ref, cache_ref, pool_ref, owner_ref, len_ref, broot_ref, rb_ref, tr_ref,
    res_ref, wo_ref, gain_ref, wq_ref,
    attn_ref, stream_ref, qkv_ref,
    kvg, wqg, qb, tok, s3, mx, mrun, acc, tags, box, part, rsb, normed, qacc,
    send1, send2, sendm, recv1, recv2, part1, part2, xsend, xrecv, swap,
):
    seq = lax.axis_index("seq")
    x = lax.axis_index("mp")
    y, z, c = seq // 16, (seq // 2) % RING, seq % 2
    scale2 = HEAD ** (-0.5) * math.log2(math.e)

    def dev(yy, zz, cc):
        return {"seq": (yy * RING + zz) * 2 + cc}

    def xdev(xx):
        return {"mp": xx}

    mate = dev(y, z, 1 - c)
    sec = (z, y)
    prim = (y, z)

    def place(h, ss, pp):
        return (pp, ss) if h == 0 else (ss, pp)

    def at(h, ss, pp):
        yy, zz = place(h, ss, pp)
        return dev(yy, zz, c)

    barrier = pltpu.get_barrier_semaphore()

    for d in (1, RING - 1):
        pl.semaphore_signal(barrier, inc=1, device_id=dev((y + d) % RING, z, c), device_id_type=MESH)
        pl.semaphore_signal(barrier, inc=1, device_id=dev(y, (z + d) % RING, c), device_id_type=MESH)
    pl.semaphore_signal(barrier, inc=1, device_id=mate, device_id_type=MESH)
    for d in range(1, 4):
        pl.semaphore_signal(barrier, inc=1, device_id=xdev((x + d) % 4), device_id_type=MESH)

    for h in range(2):
        kvg[h, seq, 0:64, :] = cache_ref[0, :, h * HEAD:(h + 1) * HEAD]
        kvg[h, seq, 64:128, :] = cache_ref[1, :, h * HEAD:(h + 1) * HEAD]
        for g in range(2):
            j = 2 * h + g
            kvg[h, seq, 128 + 16 * g:144 + 16 * g, :] = wo_ref[:, j * HEAD:(j + 1) * HEAD]
            qb[0, h, g * 64:(g + 1) * 64, :] = q_ref[:, j * HEAD:(j + 1) * HEAD]
        wqg[h, seq] = wq_ref[:, h * 512:(h + 1) * 512]

    e_id = lax.broadcasted_iota(jnp.int32, (128, 128), 0)
    b_id = lax.broadcasted_iota(jnp.int32, (128, 128), 1)
    owns = owner_ref[...] == e_id
    owned = jnp.sum(jnp.where(owns, b_id.astype(F32), 0.0), axis=1, keepdims=True)
    olen = jnp.sum(jnp.where(owns, len_ref[...].astype(F32), 0.0), axis=1, keepdims=True)
    slot = lax.broadcasted_iota(jnp.int32, (128, 32), 1).astype(F32)
    btag = jnp.where(slot < olen, ROOTS + owned, -1.0)
    pool = pool_ref[...].astype(F32).T
    tags[...] = jnp.concatenate([pool, btag, pool, btag], axis=1)
    lane = lax.broadcasted_iota(jnp.int32, (64, 128), 1)

    tr = tr_ref[...].astype(F32)
    t_id = lax.broadcasted_iota(jnp.int32, (64, 64), 0)
    u_id = lax.broadcasted_iota(jnp.int32, (64, 64), 1)
    trc = jnp.sum(jnp.where(t_id == u_id, tr, 0.0), axis=1, keepdims=True)
    rb = rb_ref[...].astype(F32)
    tb = jnp.zeros((64, 1), F32)
    for r in range(4):
        tb = jnp.where(trc == float(r), rb[:, r:r + 1], tb)
    troot = jnp.sum(
        jnp.where(tb == lane.astype(F32), broot_ref[...].astype(F32), 0.0), axis=1, keepdims=True)
    tok[0, 0] = jnp.broadcast_to(troot, (64, 128))
    tok[0, 1] = jnp.broadcast_to(tb + ROOTS, (64, 128))
    pl.semaphore_wait(barrier, 4 + 1 + 3)

    def copy1(h, yy, zz, cc, sem, to):
        ref = kvg.at[h, (yy * RING + zz) * 2 + cc]
        return pltpu.make_async_remote_copy(
            src_ref=ref, dst_ref=ref, send_sem=send1.at[h], recv_sem=sem.at[h, yy, zz],
            device_id=to, device_id_type=MESH)

    def copy2(h, yy, zz, cc, sem, to):
        ref = wqg.at[h, (yy * RING + zz) * 2 + cc]
        return pltpu.make_async_remote_copy(
            src_ref=ref, dst_ref=ref, send_sem=send2.at[h], recv_sem=sem.at[h, yy, zz],
            device_id=to, device_id_type=MESH)

    def share1(h, yy, zz, cc):
        ref = kvg.at[h, (yy * RING + zz) * 2 + cc, 128:ROWS]
        return pltpu.make_async_remote_copy(
            src_ref=ref, dst_ref=ref, send_sem=sendm.at[h], recv_sem=part1.at[h, yy, zz],
            device_id=mate, device_id_type=MESH)

    def share2(h, yy, zz, cc):
        return copy2(h, yy, zz, cc, part2, mate)

    def trade(i, mine, theirs):
        return pltpu.make_async_remote_copy(
            src_ref=mine, dst_ref=theirs, send_sem=swap.at[0, i], recv_sem=swap.at[1, i],
            device_id=mate, device_id_type=MESH)

    trades = [trade(0, qb.at[0], qb.at[1]), trade(1, tok.at[0], tok.at[1]), trade(2, box.at[0], box.at[1])]

    def inject(copy, rsem, share, h, pp):
        yy, zz = place(h, sec[h], pp)
        copy(h, yy, zz, c, rsem, at(h, (sec[h] + 1) % RING, prim[h])).start()
        copy(h, yy, zz, c, rsem, at(h, (sec[h] + RING - 1) % RING, prim[h])).start()
        share(h, yy, zz, c).start()

    def start_ring(copy, rsem):
        for h in range(2):
            for way in (1, RING - 1):
                copy(h, y, z, c, rsem, at(h, sec[h], (prim[h] + way) % RING)).start()

    start_ring(copy1, recv1)
    for h in range(2):
        inject(copy1, recv1, share1, h, prim[h])
    trades[0].start()
    trades[1].start()

    own_seen = (tr == trc) & (u_id <= t_id)
    own_seen2 = jnp.concatenate([own_seen.astype(F32), own_seen.astype(F32)], axis=0) > 0.5
    ones64 = jnp.ones((64, HEAD), BF16)
    for h in range(2):
        s = lax.dot_general(
            qb[0, h], fk_ref[:, h * HEAD:(h + 1) * HEAD], (((1,), (1,)), ((), ())),
            preferred_element_type=F32)
        s = jnp.where(own_seen2, s, NEG)
        m = jnp.max(s, axis=1, keepdims=True)
        p = jnp.exp2((s - m) * scale2).astype(BF16)
        v = jnp.concatenate([fv_ref[:, h * HEAD:(h + 1) * HEAD], ones64], axis=1)
        acc[h, 0:128] = jnp.dot(p, v, preferred_element_type=F32)
        acc[h, 128:256] = jnp.zeros((128, 256), F32)
        mrun[h, 0:128] = jnp.broadcast_to(m, (128, 128))
        mrun[h, 128:256] = jnp.full((128, 128), FLOOR, F32)
        mx[h] = jnp.full((256, 128), NEG, F32)

    def wait_same(copy, rsem, h, yy, zz):
        copy(h, yy, zz, c, rsem, mate).wait_recv()

    def ring(copy, rsem, step, after):
        for h in range(2):
            ways = (1, -1) if step < HALFRING else (1,)
            for way in ways:
                pp = (prim[h] - way * step + RING) % RING
                yy, zz = place(h, sec[h], pp)
                wait_same(copy, rsem, h, yy, zz)
                last = step == HALFRING - 1
                if step < HALFRING - 1 or (last and way == (1 if h == 0 else -1)):
                    copy(h, yy, zz, c, rsem, at(h, sec[h], (prim[h] + way + RING) % RING)).start()
                if after is not None:
                    after(h, pp)

    for step in range(1, HALFRING + 1):
        ring(copy1, recv1, step, lambda h, pp: inject(copy1, recv1, share1, h, pp))

    def near(h, i):
        d = jnp.where(i % 2 == 1, (i + 1) // 2, RING - i // 2)
        return (prim[h] + d) % RING

    def relay(copy, rsem, share, step, i):
        for h in range(2):
            b = near(h, i)
            if step == HALFRING:
                yy, zz = place(h, (sec[h] + HALFRING) % RING, b)
                wait_same(copy, rsem, h, yy, zz)
                share(h, yy, zz, c).start()
                continue
            for way in (1, -1):
                yy, zz = place(h, (sec[h] - way * step + RING) % RING, b)
                wait_same(copy, rsem, h, yy, zz)
                onward = at(h, (sec[h] + way + RING) % RING, prim[h])
                if step < HALFRING - 1:
                    copy(h, yy, zz, c, rsem, onward).start()
                else:
                    @pl.when(i % 2 == (0 if way == 1 else 1))
                    def _():
                        copy(h, yy, zz, c, rsem, onward).start()
                share(h, yy, zz, c).start()

    def bundle(h, step, i):
        if step in (0, HALFRING):
            ss = (sec[h] + step) % RING
            return [place(h, ss, near(h, 2 * i)), place(h, ss, near(h, 2 * i + 1))]
        b = near(h, i)
        return [place(h, (sec[h] - step + RING) % RING, b), place(h, (sec[h] + step) % RING, b)]

    def held(h, slots, begin):
        return jnp.concatenate(
            [kvg[h, (yy * RING + zz) * 2 + c, begin:begin + 64, :] for yy, zz in slots], axis=0)

    half_lane = lax.broadcasted_iota(jnp.int32, (1, 128), 1) < 64

    def qk(step, i):
        for h in range(2):
            slots = bundle(h, step, i)
            q = jnp.concatenate([qb[0, h], qb[1, h]], axis=0)
            s = lax.dot_general(
                q, held(h, slots, 0), (((1,), (1,)), ((), ())), preferred_element_type=F32)
            a, b = [tags[pl.ds((yy * RING + zz) * 2 + c, 1), :] for yy, zz in slots]
            tag = jnp.where(half_lane, a, b)
            parts = []
            for k in range(2):
                seen = (tag == tok[k, 0]) | (tag == tok[k, 1])
                for g in range(2):
                    r = 128 * k + 64 * g
                    parts.append(jnp.where(seen, s[r:r + 64], NEG))
            s = jnp.concatenate(parts, axis=0)
            s3[h, step * RING + i] = s
            mx[h] = jnp.maximum(mx[h], s)

    def settle():
        for h in range(2):
            old = mrun[h]
            new = jnp.maximum(old, jnp.max(mx[h], axis=1, keepdims=True))
            factor = jnp.exp2((old - new) * scale2)
            mrun[h] = new
            acc[h] = acc[h] * jnp.concatenate([factor, factor], axis=1)

    ones128 = jnp.ones((128, HEAD), BF16)

    def pv(step, i):
        for h in range(2):
            p = jnp.exp2((s3[h, step * RING + i] - mrun[h]) * scale2).astype(BF16)
            v = jnp.concatenate([held(h, bundle(h, step, i), 64), ones128], axis=1)
            acc[h] += jnp.dot(p, v, preferred_element_type=F32)

    def stage(relays, qk_step, pv_step, begin=0, end=RING):
        def body(b, carry):
            if relays is not None:
                relay(*relays, b)
            if qk_step is not None:
                qk(qk_step, b)
            if pv_step is not None:
                pv(pv_step, b)
            return carry
        lax.fori_loop(begin, end, body, 0)

    one = (copy1, recv1, share1)
    two = (copy2, recv2, share2)
    start_ring(copy2, recv2)
    trades[0].wait_recv()
    trades[1].wait_recv()
    stage((*one, 1), 0, None, 0, 4)
    stage((*one, 1), None, None, 4, RING)
    settle()
    ring(copy2, recv2, 1, None)
    stage((*one, 2), 1, 0, 0, 4)
    stage((*one, 2), 1, None, 4, RING)
    settle()
    ring(copy2, recv2, 2, None)
    stage((*one, 3), 2, 1, 0, 4)
    ring(copy2, recv2, 3, None)
    stage((*one, 3), 2, 1, 4, RING)
    settle()
    ring(copy2, recv2, 4, None)

    def inject_all(i, carry):
        for h in range(2):
            inject(*two, h, near(h, i))
        return carry

    lax.fori_loop(0, RING, inject_all, 0)
    stage((*one, 4), 3, 2)
    settle()
    stage((*two, 1), 4, 3, 0, 4)
    stage((*two, 1), None, 3, 4, RING)
    settle()
    stage(None, None, 4, 0, 4)

    lane2 = lax.broadcasted_iota(jnp.int32, (128, 128), 1) < 64
    for h in range(2):
        box[0, h, :, 0:HEAD] = acc[h, 128:256, 0:HEAD]
        box[0, h, :, HEAD:] = jnp.where(lane2, mrun[h, 128:256], acc[h, 128:256, HEAD:])
    trades[2].start()
    stage((*two, 2), None, None)
    trades[2].wait_recv()
    for h in range(2):
        m_here = mrun[h, 0:128]
        m_there = box[1, h, :, HEAD:HEAD + 1]
        top = jnp.maximum(m_here, m_there)
        w_here = jnp.exp2((m_here - top) * scale2)
        w_there = jnp.exp2((m_there - top) * scale2)
        mixed = acc[h, 0:128, 0:HEAD] * w_here + box[1, h, :, 0:HEAD] * w_there
        total = acc[h, 0:128, HEAD:] * w_here + box[1, h, :, 2 * HEAD - 1:2 * HEAD] * w_there
        a = (mixed / total).astype(BF16)
        for g in range(2):
            j = 2 * h + g
            attn_ref[:, j * HEAD:(j + 1) * HEAD] = a[g * 64:(g + 1) * 64]

    def project(yy, carry):
        for h in range(2):
            for zz in range(RING):
                share1(h, yy, zz, 1 - c).wait_recv()
        w = [kvg[h, pl.ds(yy * 16, 16), 128 + 16 * g:144 + 16 * g, :].reshape(256, HEAD)
             for h in range(2) for g in range(2)]
        t = lax.dot_general(
            attn_ref[...], jnp.concatenate(w, axis=1), (((1,), (1,)), ((), ())),
            preferred_element_type=F32)
        part[:, pl.ds(pl.multiple_of(yy * 256, 256), 256)] = t.astype(BF16)
        return carry

    lax.fori_loop(0, RING, project, 0)

    def rows(xx):
        return pl.ds(pl.multiple_of(xx * 16, 16), 16)

    def scatter(d):
        xx = (x + d) % 4
        return pltpu.make_async_remote_copy(
            src_ref=part.at[rows(xx)], dst_ref=rsb.at[4 - d - 1], send_sem=xsend.at[0, d - 1],
            recv_sem=xrecv.at[0, 4 - d - 1], device_id=xdev(xx), device_id_type=MESH)

    for d in (2, 1, 3):
        scatter(d).start()
    stage((*two, 3), None, None)
    total = part[rows(x), :].astype(F32)
    for d in range(1, 4):
        scatter(4 - d).wait_recv()
        total = total + rsb[d - 1].astype(F32)
    stream_ref[rows(x), :] = (res_ref[rows(x), :].astype(F32) + total).astype(BF16)

    def spread(d, xx):
        return pltpu.make_async_remote_copy(
            src_ref=stream_ref.at[rows(xx)], dst_ref=stream_ref.at[rows(xx)],
            send_sem=xsend.at[1, d - 1], recv_sem=xrecv.at[1, 4 - d - 1],
            device_id=xdev((x + d) % 4), device_id_type=MESH)

    for d in (2, 1, 3):
        spread(d, x).start()
    stage((*two, 4), None, None)
    for d in range(1, 4):
        spread(4 - d, (x + d) % 4).wait_recv()

    wide = stream_ref[...].astype(F32)
    mean = jnp.mean(wide * wide, axis=1, keepdims=True)
    normed[...] = (wide * lax.rsqrt(mean + 1e-06) * gain_ref[...]).astype(BF16)
    qacc[...] = jnp.zeros_like(qacc)

    def qkv(yy, carry):
        n = normed[:, pl.ds(pl.multiple_of(yy * 256, 256), 256)]
        for h in range(2):
            for zz in range(RING):
                share2(h, yy, zz, 1 - c).wait_recv()
            qacc[:, h * 512:(h + 1) * 512] += jnp.dot(
                n, wqg[h, pl.ds(yy * 16, 16)].reshape(256, 512), preferred_element_type=F32)
        return carry

    lax.fori_loop(0, RING, qkv, 0)
    qkv_ref[...] = qacc[...].astype(BF16)

    for d in range(1, 4):
        scatter(d).wait_send()
        spread(d, x).wait_send()
    for t in trades:
        t.wait_send()

    def drain(sent, sem):
        pltpu.make_async_remote_copy(
            src_ref=sent, dst_ref=sent, send_sem=sem, recv_sem=recv1.at[0, 0, 0],
            device_id=mate, device_id_type=MESH).wait_send()

    for h in range(2):
        drain(kvg.at[h, 0:63], send1.at[h])
        drain(kvg.at[h, 0:64, 128:ROWS], sendm.at[h])
        drain(wqg.at[h, 0:127], send2.at[h])


def hand_out(*refs):
    sources, results, held, sem = refs[0:3], refs[3:6], refs[6:9], refs[9]
    ins = [pltpu.make_async_copy(sources[i], held[i], sem.at[i]) for i in range(3)]
    outs = [pltpu.make_async_copy(held[i], results[i], sem.at[3 + i]) for i in range(3)]
    for copy in ins:
        copy.start()
    for i in range(3):
        ins[i].wait()
        outs[i].start()
    for copy in outs:
        copy.wait()


def on_device(
    fresh_queries, fresh_keys, fresh_values, cache, pool_root, branch_owner, branch_len,
    branch_root, request_branch, token_request, residual, wo_t, norm_gain, w_qkv,
):
    vmem = pl.BlockSpec(memory_space=pltpu.VMEM)
    args = (
        fresh_queries, fresh_keys, fresh_values, cache, pool_root.T, branch_owner.reshape(1, -1),
        branch_len.reshape(1, -1), branch_root.reshape(1, -1), request_branch, token_request,
        residual, wo_t, norm_gain.reshape(1, -1), w_qkv,
    )
    dma = pltpu.SemaphoreType.DMA
    shapes = tuple(jax.ShapeDtypeStruct((64, width), BF16) for width in (512, 2048, 1024))
    results = pl.pallas_call(
        kernel,
        out_shape=shapes,
        in_specs=[vmem] * len(args),
        out_specs=(vmem, vmem, vmem),
        scratch_shapes=[
            pltpu.VMEM((2, 2 * RING * RING, ROWS, HEAD), BF16),
            pltpu.VMEM((2, 2 * RING * RING, 16, 512), BF16),
            pltpu.VMEM((2, 2, 128, HEAD), BF16),
            pltpu.VMEM((2, 2, 64, 128), F32),
            pltpu.VMEM((2, 5 * RING, 256, 128), F32),
            pltpu.VMEM((2, 256, 128), F32),
            pltpu.VMEM((2, 256, 128), F32),
            pltpu.VMEM((2, 256, 256), F32),
            pltpu.VMEM((128, 128), F32),
            pltpu.VMEM((2, 2, 128, 256), F32),
            pltpu.VMEM((64, 2048), BF16),
            pltpu.VMEM((3, 16, 2048), BF16),
            pltpu.VMEM((64, 2048), BF16),
            pltpu.VMEM((64, 1024), F32),
            dma((2,)),
            dma((2,)),
            dma((2,)),
            dma((2, RING, RING)),
            dma((2, RING, RING)),
            dma((2, RING, RING)),
            dma((2, RING, RING)),
            dma((2, 3)),
            dma((2, 3)),
            dma((2, 3)),
        ],
        compiler_params=pltpu.CompilerParams(
            collective_id=0, has_side_effects=True, vmem_limit_bytes=60 * 1024 * 1024),
    )(*args)
    place = pl.BlockSpec(memory_space=pl.ANY)
    return pl.pallas_call(
        hand_out,
        out_shape=shapes,
        in_specs=[place] * 3,
        out_specs=(place,) * 3,
        scratch_shapes=[pltpu.VMEM(s.shape, BF16) for s in shapes] + [dma((6,))],
    )(*results)


def solution(mesh):
    return jax.shard_map(
        on_device,
        mesh=mesh,
        in_specs=(
            P("seq", "mp"),
            P("seq", "mp"),
            P("seq", "mp"),
            P(None, "seq", "mp"),
            P(),
            P(),
            P(),
            P(),
            P("seq", None),
            P("seq", None),
            P("seq", None),
            P("seq", "mp"),
            P(),
            P("seq", "mp"),
        ),
        out_specs=(P("seq", "mp"), P("seq", None), P("seq", "mp")),
        check_vma=False,
    )
```

time: 89.5 us -> 82.9 us (0.926)
  the two profiles are of different devices: /device:TPU:16 before, /device:TPU:1 now
where the time goes in v2:
time: 82.9 us; the launch traced here: 82.8 us
  Pallas kernels  82.1 us (99%)
    pallas_call x1, Pallas kernels, on_device(): pl.pallas_call(kernel, out_shape=shapes, in_specs=[vmem] * len(args), out...  80.3 us
    pallas_call x1, Pallas kernels, on_device(): pl.pallas_call(hand_out, out_shape=shapes, in_specs=[place] * 3, out_spec...  1.78 us

profile of v2, /device:TPU:1, one launch (start us, length us, event | category | flops | bytes accessed | tf_op | source)
XLA Modules:
  0.0 82.8 jit_solution(5937536026460572055)
XLA Ops:
  0.6 80.3 %shard_map.157 = (bf16[64,512]{1,0:T(8,128)(2,1)}, bf16[64,2048]{1,0:T(8,128)(2,1)}, bf16[64,1024]{1,0:T(8,128)(2,1)}) custom-call(bf16[64,512]{1,0:T(8,128)(2,1)} %q_ref.1, bf16[64,256]{1,0:T(8,128)(2,1)} %fk_ref.1, bf16[64,256]{1,0:T(8,128)(2,1)} %fv_ref.1, bf16[2,64,256]{2,1,0:T(8,128)(2,1)} %cache_ref.1, s32[32,128]{1,0:T(8,128)} %bitcast.5, ...), custom_call_target="tpu_custom_call" | custom-call | tf_op jit(solution)/shard_map/pallas_call | solution.py:412
  81.0 1.8 %shard_map.158 = (bf16[64,512]{1,0:T(8,128)(2,1)}, bf16[64,2048]{1,0:T(8,128)(2,1)}, bf16[64,1024]{1,0:T(8,128)(2,1)}) custom-call(bf16[64,512]{1,0:T(8,128)(2,1)} %get-tuple-element.6.refs_0_, bf16[64,2048]{1,0:T(8,128)(2,1)} %get-tuple-element.7.refs_1_, bf16[64,1024]{1,0:T(8,128)(2,1)} %get-tuple-element.8.refs_2_), custom_call_target="tpu_custom_call" | custom-call | tf_op jit(solution)/shard_map/pallas_call | solution.py:447

commit v3 on v2

--- a/solution.py
+++ b/solution.py
@@ -63,6 +63,58 @@
         for g in range(2):
             j = 2 * h + g
             kvg[h, seq, 128 + 16 * g:144 + 16 * g, :] = wo_ref[:, j * HEAD:(j + 1) * HEAD]
+
+    pl.semaphore_wait(barrier, 4 + 1 + 3)
+
+    def copy1(h, yy, zz, cc, sem, to):
+        ref = kvg.at[h, (yy * RING + zz) * 2 + cc]
+        return pltpu.make_async_remote_copy(
+            src_ref=ref, dst_ref=ref, send_sem=send1.at[h], recv_sem=sem.at[h, yy, zz],
+            device_id=to, device_id_type=MESH)
+
+    def copy2(h, yy, zz, cc, sem, to):
+        ref = wqg.at[h, (yy * RING + zz) * 2 + cc]
+        return pltpu.make_async_remote_copy(
+            src_ref=ref, dst_ref=ref, send_sem=send2.at[h], recv_sem=sem.at[h, yy, zz],
+            device_id=to, device_id_type=MESH)
+
+    def share1(h, yy, zz, cc):
+        ref = kvg.at[h, (yy * RING + zz) * 2 + cc, 128:ROWS]
+        return pltpu.make_async_remote_copy(
+            src_ref=ref, dst_ref=ref, send_sem=sendm.at[h], recv_sem=part1.at[h],
+            device_id=mate, device_id_type=MESH)
+
+    def share2(h, yy, zz, cc):
+        ref = wqg.at[h, (yy * RING + zz) * 2 + cc]
+        return pltpu.make_async_remote_copy(
+            src_ref=ref, dst_ref=ref, send_sem=sendm.at[2 + h], recv_sem=part2.at[h],
+            device_id=mate, device_id_type=MESH)
+
+    def trade(i, mine, theirs):
+        return pltpu.make_async_remote_copy(
+            src_ref=mine, dst_ref=theirs, send_sem=swap.at[0, i], recv_sem=swap.at[1, i],
+            device_id=mate, device_id_type=MESH)
+
+    trades = [trade(0, qb.at[0], qb.at[1]), trade(1, tok.at[0], tok.at[1]), trade(2, box.at[0, 0], box.at[1, 0]), trade(3, box.at[0, 1], box.at[1, 1])]
+
+    def inject(copy, rsem, share, h, pp):
+        yy, zz = place(h, sec[h], pp)
+        copy(h, yy, zz, c, rsem, at(h, (sec[h] + 1) % RING, prim[h])).start()
+        copy(h, yy, zz, c, rsem, at(h, (sec[h] + RING - 1) % RING, prim[h])).start()
+        share(h, yy, zz, c).start()
+
+    def start_ring(copy, rsem):
+        for h in range(2):
+            for way in (1, RING - 1):
+                copy(h, y, z, c, rsem, at(h, sec[h], (prim[h] + way) % RING)).start()
+
+    start_ring(copy1, recv1)
+    for h in range(2):
+        inject(copy1, recv1, share1, h, prim[h])
+
+    for h in range(2):
+        for g in range(2):
+            j = 2 * h + g
             qb[0, h, g * 64:(g + 1) * 64, :] = q_ref[:, j * HEAD:(j + 1) * HEAD]
         wqg[h, seq] = wq_ref[:, h * 512:(h + 1) * 512]
 
@@ -89,52 +141,9 @@
         jnp.where(tb == lane.astype(F32), broot_ref[...].astype(F32), 0.0), axis=1, keepdims=True)
     tok[0, 0] = jnp.broadcast_to(troot, (64, 128))
     tok[0, 1] = jnp.broadcast_to(tb + ROOTS, (64, 128))
-    pl.semaphore_wait(barrier, 4 + 1 + 3)
-
-    def copy1(h, yy, zz, cc, sem, to):
-        ref = kvg.at[h, (yy * RING + zz) * 2 + cc]
-        return pltpu.make_async_remote_copy(
-            src_ref=ref, dst_ref=ref, send_sem=send1.at[h], recv_sem=sem.at[h, yy, zz],
-            device_id=to, device_id_type=MESH)
-
-    def copy2(h, yy, zz, cc, sem, to):
-        ref = wqg.at[h, (yy * RING + zz) * 2 + cc]
-        return pltpu.make_async_remote_copy(
-            src_ref=ref, dst_ref=ref, send_sem=send2.at[h], recv_sem=sem.at[h, yy, zz],
-            device_id=to, device_id_type=MESH)
-
-    def share1(h, yy, zz, cc):
-        ref = kvg.at[h, (yy * RING + zz) * 2 + cc, 128:ROWS]
-        return pltpu.make_async_remote_copy(
-            src_ref=ref, dst_ref=ref, send_sem=sendm.at[h], recv_sem=part1.at[h, yy, zz],
-            device_id=mate, device_id_type=MESH)
-
-    def share2(h, yy, zz, cc):
-        return copy2(h, yy, zz, cc, part2, mate)
-
-    def trade(i, mine, theirs):
-        return pltpu.make_async_remote_copy(
-            src_ref=mine, dst_ref=theirs, send_sem=swap.at[0, i], recv_sem=swap.at[1, i],
-            device_id=mate, device_id_type=MESH)
-
-    trades = [trade(0, qb.at[0], qb.at[1]), trade(1, tok.at[0], tok.at[1]), trade(2, box.at[0], box.at[1])]
-
-    def inject(copy, rsem, share, h, pp):
-        yy, zz = place(h, sec[h], pp)
-        copy(h, yy, zz, c, rsem, at(h, (sec[h] + 1) % RING, prim[h])).start()
-        copy(h, yy, zz, c, rsem, at(h, (sec[h] + RING - 1) % RING, prim[h])).start()
-        share(h, yy, zz, c).start()
-
-    def start_ring(copy, rsem):
-        for h in range(2):
-            for way in (1, RING - 1):
-                copy(h, y, z, c, rsem, at(h, sec[h], (prim[h] + way) % RING)).start()
-
-    start_ring(copy1, recv1)
-    for h in range(2):
-        inject(copy1, recv1, share1, h, prim[h])
     trades[0].start()
     trades[1].start()
+
 
     own_seen = (tr == trc) & (u_id <= t_id)
     own_seen2 = jnp.concatenate([own_seen.astype(F32), own_seen.astype(F32)], axis=0) > 0.5
@@ -168,9 +177,6 @@
                     copy(h, yy, zz, c, rsem, at(h, sec[h], (prim[h] + way + RING) % RING)).start()
                 if after is not None:
                     after(h, pp)
-
-    for step in range(1, HALFRING + 1):
-        ring(copy1, recv1, step, lambda h, pp: inject(copy1, recv1, share1, h, pp))
 
     def near(h, i):
         d = jnp.where(i % 2 == 1, (i + 1) // 2, RING - i // 2)
@@ -196,12 +202,29 @@
                         copy(h, yy, zz, c, rsem, onward).start()
                 share(h, yy, zz, c).start()
 
-    def bundle(h, step, i):
+    one = (copy1, recv1, share1)
+    two = (copy2, recv2, share2)
+
+    def early(wave):
+        pass
+
+    start_ring(copy2, recv2)
+    for h in range(2):
+        inject(copy2, recv2, share2, h, prim[h])
+    for step in range(1, HALFRING + 1):
+        ring(copy1, recv1, step, lambda h, pp: inject(copy1, recv1, share1, h, pp))
+        early(step)
+        ring(copy2, recv2, step, lambda h, pp: inject(copy2, recv2, share2, h, pp))
+
+    def bundle(h, step, j):
         if step in (0, HALFRING):
             ss = (sec[h] + step) % RING
-            return [place(h, ss, near(h, 2 * i)), place(h, ss, near(h, 2 * i + 1))]
-        b = near(h, i)
-        return [place(h, (sec[h] - step + RING) % RING, b), place(h, (sec[h] + step) % RING, b)]
+            return [place(h, ss, near(h, 4 * j + n)) for n in range(4)]
+        return [place(h, (sec[h] + way * step + RING) % RING, near(h, 2 * j + n))
+                for n in range(2) for way in (-1, 1)]
+
+    def unit(step, j):
+        return j if step == 0 else 4 * step - 2 + j
 
     def held(h, slots, begin):
         return jnp.concatenate(
@@ -209,23 +232,26 @@
 
     half_lane = lax.broadcasted_iota(jnp.int32, (1, 128), 1) < 64
 
-    def qk(step, i):
-        for h in range(2):
-            slots = bundle(h, step, i)
+    def qk(step, j):
+        for h in range(2):
+            slots = bundle(h, step, j)
+            u = unit(step, j)
             q = jnp.concatenate([qb[0, h], qb[1, h]], axis=0)
             s = lax.dot_general(
                 q, held(h, slots, 0), (((1,), (1,)), ((), ())), preferred_element_type=F32)
-            a, b = [tags[pl.ds((yy * RING + zz) * 2 + c, 1), :] for yy, zz in slots]
-            tag = jnp.where(half_lane, a, b)
-            parts = []
+            t = [tags[pl.ds((yy * RING + zz) * 2 + c, 1), :] for yy, zz in slots]
             for k in range(2):
-                seen = (tag == tok[k, 0]) | (tag == tok[k, 1])
+                tops = [mx[h, 128 * k + 64 * g:128 * k + 64 * g + 64] for g in range(2)]
+                for n in range(2):
+                    tag = jnp.where(half_lane, t[2 * n], t[2 * n + 1])
+                    seen = (tag == tok[k, 0]) | (tag == tok[k, 1])
+                    for g in range(2):
+                        r = 128 * k + 64 * g
+                        part_s = jnp.where(seen, s[r:r + 64, 128 * n:128 * n + 128], NEG)
+                        s3[h, u, r:r + 64, 128 * n:128 * n + 128] = part_s
+                        tops[g] = jnp.maximum(tops[g], part_s)
                 for g in range(2):
-                    r = 128 * k + 64 * g
-                    parts.append(jnp.where(seen, s[r:r + 64], NEG))
-            s = jnp.concatenate(parts, axis=0)
-            s3[h, step * RING + i] = s
-            mx[h] = jnp.maximum(mx[h], s)
+                    mx[h, 128 * k + 64 * g:128 * k + 64 * g + 64] = tops[g]
 
     def settle():
         for h in range(2):
@@ -235,65 +261,54 @@
             mrun[h] = new
             acc[h] = acc[h] * jnp.concatenate([factor, factor], axis=1)
 
-    ones128 = jnp.ones((128, HEAD), BF16)
-
-    def pv(step, i):
-        for h in range(2):
-            p = jnp.exp2((s3[h, step * RING + i] - mrun[h]) * scale2).astype(BF16)
-            v = jnp.concatenate([held(h, bundle(h, step, i), 64), ones128], axis=1)
-            acc[h] += jnp.dot(p, v, preferred_element_type=F32)
-
-    def stage(relays, qk_step, pv_step, begin=0, end=RING):
-        def body(b, carry):
-            if relays is not None:
-                relay(*relays, b)
+    ones = jnp.ones((256, HEAD), BF16)
+
+    def pv(step, j, heads=(0, 1)):
+        for h in heads:
+            m = mrun[h]
+            p = jnp.exp2((s3[h, unit(step, j)] - jnp.concatenate([m, m], axis=1)) * scale2)
+            v = jnp.concatenate([held(h, bundle(h, step, j), 64), ones], axis=1)
+            acc[h] += jnp.dot(p.astype(BF16), v, preferred_element_type=F32)
+
+    def stage(relays, qk_step, pv_step, begin=0, end=HALFRING):
+        def body(j, carry):
+            for r in relays:
+                for n in range(2):
+                    relay(*r, 2 * j + n)
             if qk_step is not None:
-                qk(qk_step, b)
+                qk(qk_step, j)
             if pv_step is not None:
-                pv(pv_step, b)
+                pv(pv_step, j)
             return carry
         lax.fori_loop(begin, end, body, 0)
 
-    one = (copy1, recv1, share1)
-    two = (copy2, recv2, share2)
-    start_ring(copy2, recv2)
     trades[0].wait_recv()
     trades[1].wait_recv()
-    stage((*one, 1), 0, None, 0, 4)
-    stage((*one, 1), None, None, 4, RING)
+    stage([], 0, None, 0, 2)
     settle()
-    ring(copy2, recv2, 1, None)
-    stage((*one, 2), 1, 0, 0, 4)
-    stage((*one, 2), 1, None, 4, RING)
+    stage([(*one, 1)], 1, 0, 0, 2)
+    stage([(*one, 1)], 1, None, 2, 4)
     settle()
-    ring(copy2, recv2, 2, None)
-    stage((*one, 3), 2, 1, 0, 4)
-    ring(copy2, recv2, 3, None)
-    stage((*one, 3), 2, 1, 4, RING)
+    stage([(*one, 2)], 2, 1)
     settle()
-    ring(copy2, recv2, 4, None)
-
-    def inject_all(i, carry):
-        for h in range(2):
-            inject(*two, h, near(h, i))
-        return carry
-
-    lax.fori_loop(0, RING, inject_all, 0)
-    stage((*one, 4), 3, 2)
+    stage([(*one, 3)], 3, 2)
     settle()
-    stage((*two, 1), 4, 3, 0, 4)
-    stage((*two, 1), None, 3, 4, RING)
+    stage([(*one, 4), (*two, 1)], None, 3)
+    stage([], 4, None, 0, 2)
     settle()
-    stage(None, None, 4, 0, 4)
 
     lane2 = lax.broadcasted_iota(jnp.int32, (128, 128), 1) < 64
     for h in range(2):
+        def last(i, carry):
+            pv(4, i, (h,))
+            return carry
+        lax.fori_loop(0, 2, last, 0)
         box[0, h, :, 0:HEAD] = acc[h, 128:256, 0:HEAD]
         box[0, h, :, HEAD:] = jnp.where(lane2, mrun[h, 128:256], acc[h, 128:256, HEAD:])
-    trades[2].start()
-    stage((*two, 2), None, None)
-    trades[2].wait_recv()
-    for h in range(2):
+        trades[2 + h].start()
+    stage([(*two, 2)], None, None)
+    for h in range(2):
+        trades[2 + h].wait_recv()
         m_here = mrun[h, 0:128]
         m_there = box[1, h, :, HEAD:HEAD + 1]
         top = jnp.maximum(m_here, m_there)
@@ -306,47 +321,50 @@
             j = 2 * h + g
             attn_ref[:, j * HEAD:(j + 1) * HEAD] = a[g * 64:(g + 1) * 64]
 
-    def project(yy, carry):
-        for h in range(2):
-            for zz in range(RING):
-                share1(h, yy, zz, 1 - c).wait_recv()
-        w = [kvg[h, pl.ds(yy * 16, 16), 128 + 16 * g:144 + 16 * g, :].reshape(256, HEAD)
+    def arrived(all_of, sem):
+        pltpu.make_async_remote_copy(
+            src_ref=all_of, dst_ref=all_of, send_sem=send1.at[0], recv_sem=sem,
+            device_id=mate, device_id_type=MESH).wait_recv()
+
+    for h in range(2):
+        arrived(kvg.at[h, 0:64, 128:ROWS], part1.at[h])
+
+    def quarter(xx):
+        return pl.ds(pl.multiple_of(xx * 512, 512), 512)
+
+    def scatter(d):
+        xx = (x + d) % 4
+        return pltpu.make_async_remote_copy(
+            src_ref=part.at[:, quarter(xx)], dst_ref=rsb.at[4 - d - 1], send_sem=xsend.at[0, d - 1],
+            recv_sem=xrecv.at[0, 4 - d - 1], device_id=xdev(xx), device_id_type=MESH)
+
+    for d in (2, 1, 3, 0):
+        xx = (x + d) % 4
+        w = [kvg[h, pl.ds(xx * 32, 32), 128 + 16 * g:144 + 16 * g, :].reshape(512, HEAD)
              for h in range(2) for g in range(2)]
         t = lax.dot_general(
             attn_ref[...], jnp.concatenate(w, axis=1), (((1,), (1,)), ((), ())),
             preferred_element_type=F32)
-        part[:, pl.ds(pl.multiple_of(yy * 256, 256), 256)] = t.astype(BF16)
-        return carry
-
-    lax.fori_loop(0, RING, project, 0)
-
-    def rows(xx):
-        return pl.ds(pl.multiple_of(xx * 16, 16), 16)
-
-    def scatter(d):
-        xx = (x + d) % 4
-        return pltpu.make_async_remote_copy(
-            src_ref=part.at[rows(xx)], dst_ref=rsb.at[4 - d - 1], send_sem=xsend.at[0, d - 1],
-            recv_sem=xrecv.at[0, 4 - d - 1], device_id=xdev(xx), device_id_type=MESH)
-
-    for d in (2, 1, 3):
-        scatter(d).start()
-    stage((*two, 3), None, None)
-    total = part[rows(x), :].astype(F32)
+        part[:, quarter(xx)] = t.astype(BF16)
+        if d > 0:
+            scatter(d).start()
+
+    stage([(*two, 3)], None, None)
+    total = res_ref[:, quarter(x)].astype(F32) + part[:, quarter(x)].astype(F32)
     for d in range(1, 4):
         scatter(4 - d).wait_recv()
         total = total + rsb[d - 1].astype(F32)
-    stream_ref[rows(x), :] = (res_ref[rows(x), :].astype(F32) + total).astype(BF16)
+    stream_ref[:, quarter(x)] = total.astype(BF16)
 
     def spread(d, xx):
         return pltpu.make_async_remote_copy(
-            src_ref=stream_ref.at[rows(xx)], dst_ref=stream_ref.at[rows(xx)],
+            src_ref=stream_ref.at[:, quarter(xx)], dst_ref=stream_ref.at[:, quarter(xx)],
             send_sem=xsend.at[1, d - 1], recv_sem=xrecv.at[1, 4 - d - 1],
             device_id=xdev((x + d) % 4), device_id_type=MESH)
 
     for d in (2, 1, 3):
         spread(d, x).start()
-    stage((*two, 4), None, None)
+    stage([(*two, 4)], None, None)
     for d in range(1, 4):
         spread(4 - d, (x + d) % 4).wait_recv()
 
@@ -354,12 +372,12 @@
     mean = jnp.mean(wide * wide, axis=1, keepdims=True)
     normed[...] = (wide * lax.rsqrt(mean + 1e-06) * gain_ref[...]).astype(BF16)
     qacc[...] = jnp.zeros_like(qacc)
+    for h in range(2):
+        arrived(wqg.at[h, 0:64], part2.at[h])
 
     def qkv(yy, carry):
         n = normed[:, pl.ds(pl.multiple_of(yy * 256, 256), 256)]
         for h in range(2):
-            for zz in range(RING):
-                share2(h, yy, zz, 1 - c).wait_recv()
             qacc[:, h * 512:(h + 1) * 512] += jnp.dot(
                 n, wqg[h, pl.ds(yy * 16, 16)].reshape(256, 512), preferred_element_type=F32)
         return carry
@@ -381,18 +399,15 @@
     for h in range(2):
         drain(kvg.at[h, 0:63], send1.at[h])
         drain(kvg.at[h, 0:64, 128:ROWS], sendm.at[h])
-        drain(wqg.at[h, 0:127], send2.at[h])
+        drain(wqg.at[h, 0:63], send2.at[h])
+        drain(wqg.at[h, 0:64], sendm.at[2 + h])
 
 
 def hand_out(*refs):
-    sources, results, held, sem = refs[0:3], refs[3:6], refs[6:9], refs[9]
-    ins = [pltpu.make_async_copy(sources[i], held[i], sem.at[i]) for i in range(3)]
-    outs = [pltpu.make_async_copy(held[i], results[i], sem.at[3 + i]) for i in range(3)]
-    for copy in ins:
+    sources, results, sem = refs[0:3], refs[3:6], refs[6]
+    outs = [pltpu.make_async_copy(sources[i], results[i], sem.at[i]) for i in range(3)]
+    for copy in outs:
         copy.start()
-    for i in range(3):
-        ins[i].wait()
-        outs[i].start()
     for copy in outs:
         copy.wait()
 
@@ -411,7 +426,7 @@
     shapes = tuple(jax.ShapeDtypeStruct((64, width), BF16) for width in (512, 2048, 1024))
     results = pl.pallas_call(
         kernel,
-        out_shape=shapes,
+        out_shape=tuple(pltpu.VMEM(s.shape, BF16) for s in shapes),
         in_specs=[vmem] * len(args),
         out_specs=(vmem, vmem, vmem),
         scratch_shapes=[
@@ -419,38 +434,31 @@
             pltpu.VMEM((2, 2 * RING * RING, 16, 512), BF16),
             pltpu.VMEM((2, 2, 128, HEAD), BF16),
             pltpu.VMEM((2, 2, 64, 128), F32),
-            pltpu.VMEM((2, 5 * RING, 256, 128), F32),
+            pltpu.VMEM((2, 2 * RING, 256, 256), F32),
             pltpu.VMEM((2, 256, 128), F32),
             pltpu.VMEM((2, 256, 128), F32),
             pltpu.VMEM((2, 256, 256), F32),
             pltpu.VMEM((128, 128), F32),
             pltpu.VMEM((2, 2, 128, 256), F32),
             pltpu.VMEM((64, 2048), BF16),
-            pltpu.VMEM((3, 16, 2048), BF16),
+            pltpu.VMEM((3, 64, 512), BF16),
             pltpu.VMEM((64, 2048), BF16),
             pltpu.VMEM((64, 1024), F32),
             dma((2,)),
             dma((2,)),
-            dma((2,)),
+            dma((4,)),
             dma((2, RING, RING)),
             dma((2, RING, RING)),
-            dma((2, RING, RING)),
-            dma((2, RING, RING)),
+            dma((2,)),
+            dma((2,)),
             dma((2, 3)),
             dma((2, 3)),
-            dma((2, 3)),
+            dma((2, 4)),
         ],
         compiler_params=pltpu.CompilerParams(
             collective_id=0, has_side_effects=True, vmem_limit_bytes=60 * 1024 * 1024),
     )(*args)
-    place = pl.BlockSpec(memory_space=pl.ANY)
-    return pl.pallas_call(
-        hand_out,
-        out_shape=shapes,
-        in_specs=[place] * 3,
-        out_specs=(place,) * 3,
-        scratch_shapes=[pltpu.VMEM(s.shape, BF16) for s in shapes] + [dma((6,))],
-    )(*results)
+    return tuple(results)
 
 
 def solution(mesh):

time: 82.9 us -> 73.4 us (0.89); the launches traced: 82.8 us -> 72.2 us
  Pallas kernels: 82.1 us -> 69.5 us
  local copies, waits for them, and re-layouts: 0 us -> 1.99 us
    pallas_call x2 -> x1, Pallas kernels: 82.1 us -> 69.5 us  [on_device(): pl.pallas_call(kernel, out_shape=tuple((pltpu.VMEM(s.shape, BF16) for s i...]
    unnamed x0 -> x3, local copies, waits for them, and re-layouts: none -> 1.99 us
where the time goes in v3:
time: 73.4 us; the launch traced here: 72.2 us
  Pallas kernels  69.5 us (95%)
  local copies, waits for them, and re-layouts  1.99 us (3%)
    pallas_call x1, Pallas kernels, on_device(): pl.pallas_call(kernel, out_shape=tuple((pltpu.VMEM(s.shape, BF16) for s i...  69.5 us
    unnamed x3, local copies, waits for them, and re-layouts  1.99 us

profile of v3, /device:TPU:1, one launch (start us, length us, event | category | flops | bytes accessed | tf_op | source)
XLA Modules:
  0.0 72.2 jit_solution(7510891783539841639)
XLA Ops:
  0.6 69.5 %shard_map.157 = (bf16[64,512]{1,0:T(8,128)(2,1)S(1)}, bf16[64,2048]{1,0:T(8,128)(2,1)S(1)}, bf16[64,1024]{1,0:T(8,128)(2,1)S(1)}) custom-call(bf16[64,512]{1,0:T(8,128)(2,1)} %q_ref.1, bf16[64,256]{1,0:T(8,128)(2,1)} %fk_ref.1, bf16[64,256]{1,0:T(8,128)(2,1)} %fv_ref.1, bf16[2,64,256]{2,1,0:T(8,128)(2,1)} %cache_ref.1, s32[32,128]{1,0:T(8,128)} %bitcast.5, ...), custom_call_target="tpu_custom_call" | custom-call | tf_op jit(solution)/shard_map/pallas_call | solution.py:427
  70.2 0.6 copy.20
  70.8 0.7 copy.22
  71.5 0.7 copy.21

commit v4 on v3

--- a/solution.py
+++ b/solution.py
@@ -206,7 +206,14 @@
     two = (copy2, recv2, share2)
 
     def early(wave):
-        pass
+        if wave == 2:
+            relay(*one, 1, 0)
+            relay(*one, 1, 1)
+        if wave == 3:
+            relay(*one, 1, 2)
+            relay(*one, 1, 3)
+            relay(*one, 2, 0)
+            relay(*one, 2, 1)
 
     start_ring(copy2, recv2)
     for h in range(2):
@@ -286,10 +293,11 @@
     trades[1].wait_recv()
     stage([], 0, None, 0, 2)
     settle()
-    stage([(*one, 1)], 1, 0, 0, 2)
     stage([(*one, 1)], 1, None, 2, 4)
+    stage([], 1, 0, 0, 2)
     settle()
-    stage([(*one, 2)], 2, 1)
+    stage([(*one, 2)], 2, 1, 1, 4)
+    stage([], 2, 1, 0, 1)
     settle()
     stage([(*one, 3)], 3, 2)
     settle()
@@ -376,13 +384,13 @@
         arrived(wqg.at[h, 0:64], part2.at[h])
 
     def qkv(yy, carry):
-        n = normed[:, pl.ds(pl.multiple_of(yy * 256, 256), 256)]
+        n = normed[:, quarter(yy)]
         for h in range(2):
             qacc[:, h * 512:(h + 1) * 512] += jnp.dot(
-                n, wqg[h, pl.ds(yy * 16, 16)].reshape(256, 512), preferred_element_type=F32)
+                n, wqg[h, pl.ds(yy * 32, 32)].reshape(512, 512), preferred_element_type=F32)
         return carry
 
-    lax.fori_loop(0, RING, qkv, 0)
+    lax.fori_loop(0, 4, qkv, 0)
     qkv_ref[...] = qacc[...].astype(BF16)
 
     for d in range(1, 4):

time: 73.4 us -> 72.3 us (0.985)
  Pallas kernels: 69.5 us -> 68.4 us
    pallas_call x1, Pallas kernels: 69.5 us -> 68.4 us  [on_device(): pl.pallas_call(kernel, out_shape=tuple((pltpu.VMEM(s.shape, BF16) for s i...]
where the time goes in v4:
time: 72.3 us; the launch traced here: 71 us
  Pallas kernels  68.4 us (95%)
  local copies, waits for them, and re-layouts  1.99 us (3%)
    pallas_call x1, Pallas kernels, on_device(): pl.pallas_call(kernel, out_shape=tuple((pltpu.VMEM(s.shape, BF16) for s i...  68.4 us
    unnamed x3, local copies, waits for them, and re-layouts  1.99 us

profile of v4, /device:TPU:1, one launch (start us, length us, event | category | flops | bytes accessed | tf_op | source)
XLA Modules:
  0.0 71.0 jit_solution(632862211343693927)
XLA Ops:
  0.6 68.4 %shard_map.157 = (bf16[64,512]{1,0:T(8,128)(2,1)S(1)}, bf16[64,2048]{1,0:T(8,128)(2,1)S(1)}, bf16[64,1024]{1,0:T(8,128)(2,1)S(1)}) custom-call(bf16[64,512]{1,0:T(8,128)(2,1)} %q_ref.1, bf16[64,256]{1,0:T(8,128)(2,1)} %fk_ref.1, bf16[64,256]{1,0:T(8,128)(2,1)} %fv_ref.1, bf16[2,64,256]{2,1,0:T(8,128)(2,1)} %cache_ref.1, s32[32,128]{1,0:T(8,128)} %bitcast.5, ...), custom_call_target="tpu_custom_call" | custom-call | tf_op jit(solution)/shard_map/pallas_call | solution.py:435
  69.0 0.6 copy.20
  69.7 0.7 copy.22
  70.3 0.7 copy.21

commit v5 on v4

--- a/solution.py
+++ b/solution.py
@@ -23,7 +23,7 @@
     q_ref, fk_ref, fv_ref, cache_ref, pool_ref, owner_ref, len_ref, broot_ref, rb_ref, tr_ref,
     res_ref, wo_ref, gain_ref, wq_ref,
     attn_ref, stream_ref, qkv_ref,
-    kvg, wqg, qb, tok, s3, mx, mrun, acc, tags, box, part, rsb, normed, qacc,
+    kvg, wqg, qb, tok, s3, mx, mrun, acc, tags, box, part, rsb, normed,
     send1, send2, sendm, recv1, recv2, part1, part2, xsend, xrecv, swap,
 ):
     seq = lax.axis_index("seq")
@@ -379,19 +379,16 @@
     wide = stream_ref[...].astype(F32)
     mean = jnp.mean(wide * wide, axis=1, keepdims=True)
     normed[...] = (wide * lax.rsqrt(mean + 1e-06) * gain_ref[...]).astype(BF16)
-    qacc[...] = jnp.zeros_like(qacc)
     for h in range(2):
         arrived(wqg.at[h, 0:64], part2.at[h])
 
-    def qkv(yy, carry):
-        n = normed[:, quarter(yy)]
-        for h in range(2):
-            qacc[:, h * 512:(h + 1) * 512] += jnp.dot(
-                n, wqg[h, pl.ds(yy * 32, 32)].reshape(512, 512), preferred_element_type=F32)
-        return carry
-
-    lax.fori_loop(0, 4, qkv, 0)
-    qkv_ref[...] = qacc[...].astype(BF16)
+    for h in range(2):
+        sums = jnp.zeros((64, 512), F32)
+        for yy in range(4):
+            sums = sums + jnp.dot(
+                normed[:, yy * 512:(yy + 1) * 512], wqg[h, yy * 32:(yy + 1) * 32].reshape(512, 512),
+                preferred_element_type=F32)
+        qkv_ref[:, h * 512:(h + 1) * 512] = sums.astype(BF16)
 
     for d in range(1, 4):
         scatter(d).wait_send()
@@ -451,7 +448,6 @@
             pltpu.VMEM((64, 2048), BF16),
             pltpu.VMEM((3, 64, 512), BF16),
             pltpu.VMEM((64, 2048), BF16),
-            pltpu.VMEM((64, 1024), F32),
             dma((2,)),
             dma((2,)),
             dma((4,)),

time: 72.3 us -> 71.9 us (level)
  no operation moved by 1% of the time
where the time goes in v5:
time: 71.9 us; the launch traced here: 70.7 us
  Pallas kernels  68 us (95%)
  local copies, waits for them, and re-layouts  1.99 us (3%)
    pallas_call x1, Pallas kernels, on_device(): pl.pallas_call(kernel, out_shape=tuple((pltpu.VMEM(s.shape, BF16) for s i...  68 us
    unnamed x3, local copies, waits for them, and re-layouts  1.99 us

profile of v5, /device:TPU:1, one launch (start us, length us, event | category | flops | bytes accessed | tf_op | source)
XLA Modules:
  0.0 70.7 jit_solution(5977341099513446078)
XLA Ops:
  0.6 68.0 %shard_map.157 = (bf16[64,512]{1,0:T(8,128)(2,1)S(1)}, bf16[64,2048]{1,0:T(8,128)(2,1)S(1)}, bf16[64,1024]{1,0:T(8,128)(2,1)S(1)}) custom-call(bf16[64,512]{1,0:T(8,128)(2,1)} %q_ref.1, bf16[64,256]{1,0:T(8,128)(2,1)} %fk_ref.1, bf16[64,256]{1,0:T(8,128)(2,1)} %fv_ref.1, bf16[2,64,256]{2,1,0:T(8,128)(2,1)} %cache_ref.1, s32[32,128]{1,0:T(8,128)} %bitcast.5, ...), custom_call_target="tpu_custom_call" | custom-call | tf_op jit(solution)/shard_map/pallas_call | solution.py:432
  68.7 0.6 copy.20
  69.3 0.7 copy.22
  70.0 0.7 copy.21
